TPU v7x, 512 devices: a whole 4x4x16 slice. The times are simulated.
512 devices in a mesh: row: 16 (over y, x), col: 32 (over z, core).
Axes of the slice: x: 4, y: 4, z: 16, core: 2. Of those that a mesh axis runs over, the one named last changes fastest.
Arguments:
- panel: bfloat16 [4, 16, 512, 512], P(None, 'row', 'col'), may hold values from -1.1953125 to 1.1953125
- inverse_factor: bfloat16 [512, 512], replicated
- slot_rows: int32 [16, 32, 2], P('row', 'col'), may hold values from 0 to 63, as said below
- slot_cols: int32 [16, 32, 2], P('row', 'col'), may hold values from 0 to 63, as said below
- live_count: int32 [16, 32], P('row', 'col'), may hold values from 0 to 2
Outputs:
- contrib: bfloat16 [16, 32, 2, 512, 512], P('row', 'col')
Inputs may be any that keep to these rules, and one draw needn't show every extreme that they name: slot_rows[r, c, s] is congruent to r modulo 16; for s < live_count[r, c] the slots of one position name distinct blocks with slot_rows >= slot_cols; the other slots are ignored. slot_cols[r, c, s] is congruent to c modulo 32.
All inputs are finite; a program needn't handle non-finite values.
Results may differ from a plain program's by a relative error of at most 0.0054.
Values may be sent and summed in bfloat16 or wider, within the bound.
No kernel may reach another device: no remote copies, remote signals or barrier semaphores. Data moves between devices by JAX's collectives and lax.ppermute only.
A program may use at most 64 MiB of HBM per device.

v0:
```python
import jax
import jax.numpy as jnp
from jax import lax
from jax.sharding import PartitionSpec as P


def broadcast(value, axis, source):
    kept = jnp.where(lax.axis_index(axis) == source, value, 0).astype(value.dtype)
    return lax.psum(kept, axis)


def body(panel, inverse_factor, slot_rows, slot_cols, live_count):
    panel_count, _, part_rows, tile_width = panel.shape
    grid_rows = lax.axis_size("row")
    grid_cols = lax.axis_size("col")
    col_ratio = grid_cols // grid_rows
    column_count = panel_count // col_ratio
    solved = jnp.dot(
        panel.reshape(-1, tile_width), inverse_factor, preferred_element_type=jnp.float32
    )
    solved = solved.astype(jnp.bfloat16).reshape(panel_count, 1, part_rows, tile_width)
    row_blocks = lax.all_gather(solved, "col", axis=2, tiled=True).reshape(
        panel_count, tile_width, tile_width
    )
    position = lax.axis_index("col")
    grouped = row_blocks.reshape(column_count, col_ratio, tile_width, tile_width)
    picked = lax.dynamic_index_in_dim(grouped, position // grid_rows, 1, keepdims=False)
    col_blocks = broadcast(picked, "row", position % grid_rows)
    slot_total = slot_rows.shape[-1]
    rows_here = slot_rows.reshape(-1)
    cols_here = slot_cols.reshape(-1)
    live_here = live_count.reshape(())
    result = jnp.zeros((slot_total, tile_width, tile_width), jnp.bfloat16)

    def update(slot, current):
        left_tile = lax.dynamic_index_in_dim(
            row_blocks, rows_here[slot] // grid_rows, 0, keepdims=False
        )
        right_tile = lax.dynamic_index_in_dim(
            col_blocks, cols_here[slot] // grid_cols, 0, keepdims=False
        )
        product = lax.dot_general(
            left_tile, right_tile, (((1,), (1,)), ((), ())), preferred_element_type=jnp.float32
        )
        return lax.dynamic_update_index_in_dim(current, (-product).astype(jnp.bfloat16), slot, 0)

    result = lax.fori_loop(0, live_here, update, result)
    return result.reshape(1, 1, slot_total, tile_width, tile_width)


def solution(mesh):
    placed = (
        P(None, "row", "col", None),
        P(),
        P("row", "col", None),
        P("row", "col", None),
        P("row", "col"),
    )
    return jax.shard_map(
        body,
        mesh=mesh,
        in_specs=placed,
        out_specs=P("row", "col", None, None, None),
        check_vma=False,
    )
```

profile of v0, /device:TPU:2, one launch (start us, length us, event | category | flops | bytes accessed | tf_op | source)
XLA Modules:
  0.0 229.4 jit_solution(7024908279362446910)
XLA Ops:
  6.5 0.0 copy-start
  6.5 0.0 all-gather.2.cloned.1.call-start
  6.5 1.0 copy-done
  7.6 1.7 convolution_convert_fusion
  9.3 0.0 all-gather.2.cloned.1.call-update
  9.3 0.0 all-reduce.2.cloned.1.call-start
  9.4 76.5 %all-gather.2.cloned.1.call-done = bf16[4,1,512,512]{3,2,0,1:T(8,128)(2,1)} async-done(((bf16[4,1,16,512]{3,2,0,1:T(8,128)(2,1)}), bf16[4,1,512,512]{3,2,0,1:T(8,128)(2,1)}) %all-gather.2.cloned.1.call-update) | async-done | bytes 2097168 | tf_op jit(solution)/shard_map/all_gather | solution.py:22
  85.8 0.0 copy-start.2
  85.8 0.0 copy-start.3
  85.8 2.3 select_bitcast_fusion
  88.1 0.0 all-reduce.2.cloned.1.call-update
  88.1 115.3 %all-reduce.2.cloned.1.call-done = bf16[2,512,512]{2,1,0:T(8,128)(2,1)} async-done(((bf16[2,512,512]{2,1,0:T(8,128)(2,1)}), bf16[2,512,512]{2,1,0:T(8,128)(2,1)}) %all-reduce.2.cloned.1.call-update) | async-done | bytes 1048592 | tf_op jit(solution)/shard_map/psum | solution.py:9
  203.4 0.1 broadcast_in_dim.15
  203.5 0.0 copy-done.2
  203.5 0.0 copy-done.3
  203.5 18.1 %while.13 = (s32[]{:T(128)}, bf16[2,512,512]{2,1,0:T(8,128)(2,1)S(1)}, s32[]{:T(128)}, s32[2]{0:T(128)S(1)}, bf16[4,512,512]{2,1,0:T(8,128)(2,1)}, /*index=5*/s3...) while((s32[]{:T(128)}, ...), condition=%wide.region_2.3_spmd, body=%wide.region_1.2_spmd.sunk | while | flops 268959776 | bytes 1573451 | solution.py:47
  204.2 0.6 dynamic_slice.51
  207.4 0.6 dynamic_slice.50
  210.6 1.7 fusion.15
  212.9 0.6 dynamic_slice.51
  216.1 0.6 dynamic_slice.50
  219.3 1.7 fusion.15
  221.6 0.0 copy-start.1
  221.6 1.0 copy-done.1
Async XLA Ops:
  6.5 1.0 copy-start
  6.5 79.3 %all-gather.2.cloned.1.call-start = ((), (), s32[]{:S(2)}) async-start(), calls=%async_computation | async-start | bytes 2162688 | tf_op jit(solution)/shard_map/all_gather | solution.py:22
  9.3 194.1 %all-reduce.2.cloned.1.call-start = ((), (), s32[]{:S(2)}) async-start(), calls=%async_computation.1 | async-start | bytes 2097152 | tf_op jit(solution)/shard_map/psum | solution.py:9
  85.8 117.7 %copy-start.2 = (s32[1,1,2]{2,1,0:T(1,128)S(1)}, s32[1,1,2]{2,1,0:T(1,128)}, u32[]{:S(2)}) copy-start(s32[1,1,2]{2,1,0:T(1,128)} %param.9) | copy-start | bytes 28
  85.8 117.7 %copy-start.3 = (s32[1,1,2]{2,1,0:T(1,128)S(1)}, s32[1,1,2]{2,1,0:T(1,128)}, u32[]{:S(2)}) copy-start(s32[1,1,2]{2,1,0:T(1,128)} %param.10) | copy-start | bytes 28
  221.6 1.0 copy-start.1
Sparse Core Ops, SparseCore 0:
  9.5 76.2 all-gather.1
  89.1 114.2 all-reduce.1
where the time goes:
time: 230 us; the launch traced here: 229 us
  waiting for transfers between devices  192 us (83%)
  between operations  13.5 us (6%)
  loops' own time  12.4 us (5%)
  matrix products  5.02 us (2%)
  local copies, waits for them, and re-layouts  4.43 us (2%)
    psum x1, waiting for transfers between devices, broadcast(): return lax.psum(kept, axis)  115 us
    all_gather x1, waiting for transfers between devices, body(): lax.all_gather(solved, 'col', axis=2, tiled=True)  76.5 us
    another operation x1, loops' own time, body(): result = lax.fori_loop(0, live_here, update, result)  12.4 us
  transfers between devices with their start and end apart: 2, of which 2 were waited for; matrix products, arithmetic and copies ran while one was open for 0% of the time, Pallas kernels for 0%

commit v1 on v0

v1 whole, which is shorter than its diff:
```python
import functools

import jax
import jax.numpy as jnp
from jax import lax
from jax.experimental import pallas as pl
from jax.experimental.pallas import tpu as pltpu
from jax.sharding import PartitionSpec as P

STEPS = (
    ((4, (0,)), (-4, (0,)), (8, (0,))),
    ((1, (0, -4, 4, 8)), (-1, (0, -4, 4, 8)), (2, (0, 8)), (-2, (0, 8))),
)
CHIPS = 16


def norm(offset):
    return (offset + 7) % CHIPS - 7


def shift_z(value, shift):
    size = 2 * CHIPS
    return lax.ppermute(value, "col", [(i, (i + 2 * shift) % size) for i in range(size)])


def swap_core(value):
    return lax.ppermute(value, "col", [(i, i ^ 1) for i in range(2 * CHIPS)])


def gather_left(piece):
    have = {0: piece}
    groups = [((0,), piece[None])]
    out = []
    for number, step in enumerate(STEPS):
        fresh, names, parts = {}, [], []
        for shift, offsets in step:
            sent = jnp.stack([have[o] for o in offsets])
            got = shift_z(sent, shift)
            for index, o in enumerate(offsets):
                name = norm(o - shift)
                if name not in have and name not in fresh:
                    fresh[name] = got[index]
                    names.append(name)
                    parts.append(got[index])
        have.update(fresh)
        if number == 0:
            names, parts = [0] + names, [piece] + parts
        group = jnp.stack(parts)
        out.append((tuple(names), group, swap_core(group)))
    return out


def gather_right(piece):
    rows = lax.axis_size("row")
    col = lax.axis_index("col")
    pair = piece.reshape(2, 2, *piece.shape[1:])
    got = []
    for k in range(2):
        half = (col + k) % 2
        sent = lax.dynamic_index_in_dim(pair, half, 1, keepdims=False)
        perm = [
            (r * 32 + c, (c // 2) * 32 + r + rows * ((c + k) % 2))
            for r in range(rows)
            for c in range(32)
        ]
        got.append(lax.ppermute(sent, ("row", "col"), perm))
    high = col // rows == 1
    both = jnp.stack(
        [jnp.where(high, got[1], got[0]), jnp.where(high, got[0], got[1])]
    )
    spread = jnp.broadcast_to(both[None], (rows, *both.shape))
    return lax.all_to_all(spread, "row", 0, 0, tiled=True)


def kernel(names, rows_ref, cols_ref, live_ref, w_ref, right_ref, *refs):
    lefts, out_ref, a_ref, f_ref = refs[:-3], refs[-3], refs[-2], refs[-1]
    col = lax.axis_index("col")
    z = lax.div(col, 2)
    core = lax.rem(col, 2)
    live = live_ref[0, 0]
    w = w_ref[...]
    size = w.shape[0]
    dims = (((1,), (1,)), ((), ()))
    for b in range(2):
        block = right_ref[:, :, b].reshape(size, size)
        f_ref[b] = jnp.dot(block, w, preferred_element_type=jnp.float32).astype(jnp.bfloat16)
    for slot in range(2):

        @pl.when(slot < live)
        def _():
            a = rows_ref[0, 0, slot] // 16
            b = cols_ref[0, 0, slot] // 32
            for group, offsets in enumerate(names):
                for index, offset in enumerate(offsets):
                    origin = lax.rem(z + offset + CHIPS, CHIPS)
                    for other in range(2):
                        who = core if other == 0 else 1 - core
                        start = pl.multiple_of((2 * origin + who) * 16, 16)
                        a_ref[pl.ds(start, 16), :] = lefts[2 * group + other][index, a]
            left = jnp.dot(a_ref[...], w, preferred_element_type=jnp.float32).astype(jnp.bfloat16)
            product = lax.dot_general(left, f_ref[b], dims, preferred_element_type=jnp.float32)
            out_ref[slot] = (-product).astype(jnp.bfloat16)

        @pl.when(slot >= live)
        def _():
            out_ref[slot] = jnp.zeros_like(out_ref[slot])


def body(panel, inverse_factor, slot_rows, slot_cols, live_count):
    piece = panel[:, 0]
    size = inverse_factor.shape[0]
    right = gather_right(piece)
    groups = gather_left(piece)
    names = tuple(g[0] for g in groups)
    lefts = [array for g in groups for array in g[1:]]
    smem = pl.BlockSpec(memory_space=pltpu.SMEM)
    vmem = pl.BlockSpec(memory_space=pltpu.VMEM)
    out = pl.pallas_call(
        functools.partial(kernel, names),
        out_shape=jax.ShapeDtypeStruct((2, size, size), jnp.bfloat16),
        in_specs=[smem] * 3 + [vmem] * (2 + len(lefts)),
        out_specs=vmem,
        scratch_shapes=[
            pltpu.VMEM((size, size), jnp.bfloat16),
            pltpu.VMEM((2, size, size), jnp.bfloat16),
        ],
        compiler_params=pltpu.CompilerParams(vmem_limit_bytes=32 * 2**20),
    )(slot_rows, slot_cols, live_count, inverse_factor, right, *lefts)
    return out[None, None]


def solution(mesh):
    placed = (
        P(None, "row", "col", None),
        P(),
        P("row", "col", None),
        P("row", "col", None),
        P("row", "col"),
    )
    return jax.shard_map(
        body,
        mesh=mesh,
        in_specs=placed,
        out_specs=P("row", "col", None, None, None),
        check_vma=False,
    )
```

time: 230 us -> 83.8 us (0.36)
  the two profiles are of different devices: /device:TPU:2 before, /device:TPU:1 now
where the time goes in v1:
time: 83.8 us; the launch traced here: 83.3 us
  starting transfers between devices  69.8 us (83%)
  waiting for transfers between devices  5.84 us (7%)
  Pallas kernels  3.75 us (4%)
  local copies, waits for them, and re-layouts  2.83 us (3%)
  between operations  0.97 us (1%)
    ppermute x7, starting transfers between devices, shift_z(): lax.ppermute(value, 'col', [(i, (i + 2 * shift) % size) for i in range(si...  46.1 us
    ppermute x2, starting transfers between devices, gather_right(): got.append(lax.ppermute(sent, ('row', 'col'), perm))  9.96 us
    all_to_all x1, starting transfers between devices, gather_right(): return lax.all_to_all(spread, 'row', 0, 0, tiled=True)  9.39 us
    ppermute x7, waiting for transfers between devices, shift_z(): lax.ppermute(value, 'col', [(i, (i + 2 * shift) % size) for i in range(si...  4.99 us
    ppermute x2, starting transfers between devices, swap_core(): return lax.ppermute(value, 'col', [(i, i ^ 1) for i in range(2 * CHIPS)])  4.33 us
    pallas_call x1, Pallas kernels, body(): pl.pallas_call(functools.partial(kernel, names), out_shape=jax.ShapeDtype...  3.75 us
    unnamed x15, local copies, waits for them, and re-layouts  1.71 us
  transfers between devices with their start and end apart: 12, of which 3 were waited for; matrix products, arithmetic and copies ran while one was open for 1% of the time, Pallas kernels for 0%

profile of v1, /device:TPU:1, one launch (start us, length us, event | category | flops | bytes accessed | tf_op | source)
XLA Modules:
  0.0 83.3 jit_solution(16328254508664281814)
XLA Ops:
  0.0 0.0 copy-start.5
  0.0 16.4 %collective-permute-start.4 = (bf16[1,4,16,512]{3,2,1,0:T(8,128)(2,1)}, bf16[1,4,16,512]{3,2,1,0:T(8,128)(2,1)S(1)}, u32[]{:S(2)}, u32[]{:S(2)}) collective-permute-start(bf16[1,4,16,512]{3,2,1,0:T(8,128)(2,1)} %bitcast.11), channel_id=1, source_target_pairs={{0,16},{1,17},{2,18},{3,19},{4,20},{5,21},{6,22},{7,23},{8,24},{9,... | collective-permute-start | bytes 196616 | tf_op jit(solution)/shard_map/ppermute | solution.py:23
  16.4 4.0 %collective-permute-start.2 = (bf16[1,4,16,512]{3,2,1,0:T(8,128)(2,1)}, bf16[1,4,16,512]{3,2,1,0:T(8,128)(2,1)S(1)}, u32[]{:S(2)}, u32[]{:S(2)}) collective-permute-start(bf16[1,4,16,512]{3,2,1,0:T(8,128)(2,1)} %bitcast.12), channel_id=1, source_target_pairs={{0,8},{1,9},{2,10},{3,11},{4,12},{5,13},{6,14},{7,15},{8,16},{9,17... | collective-permute-start | bytes 196616 | tf_op jit(solution)/shard_map/ppermute | solution.py:23
  20.4 5.2 %collective-permute-start.3 = (bf16[1,4,16,512]{3,2,1,0:T(8,128)(2,1)}, bf16[1,4,16,512]{3,2,1,0:T(8,128)(2,1)S(1)}, u32[]{:S(2)}, u32[]{:S(2)}) collective-permute-start(bf16[1,4,16,512]{3,2,1,0:T(8,128)(2,1)} %bitcast.13), channel_id=1, source_target_pairs={{0,24},{1,25},{2,26},{3,27},{4,28},{5,29},{6,30},{7,31},{8,0},{9,1... | collective-permute-start | bytes 196616 | tf_op jit(solution)/shard_map/ppermute | solution.py:23
  25.6 0.0 copy-done.5
  25.7 3.4 %collective-permute-start = (bf16[2,16,512]{2,1,0:T(8,128)(2,1)S(1)}, bf16[2,16,512]{2,1,0:T(8,128)(2,1)S(1)}, u32[]{:S(2)}, u32[]{:S(2)}) collective-permute-start(bf16[2,16,512]{2,1,0:T(8,128)(2,1)S(1)} %get-tuple-element.7), channel_id=1, source_target_pairs={{0,16},{1,0},{2,48},{3,32},{4,80},{5,64},{6,112},{7,96},{8,144},{9... | collective-permute-start | bytes 98312 | tf_op jit(solution)/shard_map/ppermute | solution.py:66
  29.1 6.5 %collective-permute-start.1 = (bf16[2,16,512]{2,1,0:T(8,128)(2,1)S(1)}, bf16[2,16,512]{2,1,0:T(8,128)(2,1)S(1)}, u32[]{:S(2)}, u32[]{:S(2)}) collective-permute-start(bf16[2,16,512]{2,1,0:T(8,128)(2,1)S(1)} %get-tuple-element.8), channel_id=1, source_target_pairs={{0,0},{1,16},{2,32},{3,48},{4,64},{5,80},{6,96},{7,112},{8,128},{9... | collective-permute-start | bytes 98312 | tf_op jit(solution)/shard_map/ppermute | solution.py:66
  35.7 0.0 collective-permute-done.4
  35.7 0.0 collective-permute-done.2
  35.7 0.0 collective-permute-done.3
  35.7 2.0 %collective-permute-start.6 = (bf16[4,4,16,512]{3,2,1,0:T(8,128)(2,1)S(1)}, bf16[4,4,16,512]{3,2,1,0:T(8,128)(2,1)S(1)}, u32[]{:S(2)}, u32[]{:S(2)}) collective-permute-start(bf16[4,4,16,512]{3,2,1,0:T(8,128)(2,1)S(1)} %pad_maximum_fusion.refs_0_), channel_id=1, source_target_pairs={{0,2},{1,3},{2,4},{3,5},{4,6},{5,7},{6,8},{7,9},{8,10},{9,11},{10,... | collective-permute-start | bytes 786440 | tf_op jit(solution)/shard_map/ppermute | solution.py:23
  37.7 0.0 collective-permute-done
  37.7 0.0 collective-permute-done.1
  37.8 11.2 %collective-permute-start.7 = (bf16[4,4,16,512]{3,2,1,0:T(8,128)(2,1)S(1)}, bf16[4,4,16,512]{3,2,1,0:T(8,128)(2,1)S(1)}, u32[]{:S(2)}, u32[]{:S(2)}) collective-permute-start(bf16[4,4,16,512]{3,2,1,0:T(8,128)(2,1)S(1)} %pad_maximum_fusion.refs_0_), channel_id=1, source_target_pairs={{0,30},{1,31},{2,0},{3,1},{4,2},{5,3},{6,4},{7,5},{8,6},{9,7},{10,... | collective-permute-start | bytes 786440 | tf_op jit(solution)/shard_map/ppermute | solution.py:23
  49.0 1.1 %broadcast_in_dim.4 = bf16[16,2,2,16,512]{4,3,2,1,0:T(8,128)(2,1)} broadcast(bf16[2,2,16,512]{3,2,1,0:T(8,128)(2,1)S(1)} %pad_maximum_fusion.2), dimensions={1,2,3,4} | broadcast | bytes 1114112 | tf_op jit(solution)/shard_map/broadcast_in_dim | solution.py:71
  50.1 9.4 %all-to-all-start = ((bf16[16,2,2,16,512]{4,3,2,1,0:T(8,128)(2,1)}), bf16[16,2,2,16,512]{4,3,2,1,0:T(8,128)(2,1)S(1)}, u32[]{:S(2)}, u32[]{:S(2)}) async-start(bf16[16,2,2,16,512]{4,3,2,1,0:T(8,128)(2,1)} %broadcast_in_dim.4), calls=%async_computation | async-start | bytes 2097152 | tf_op jit(solution)/shard_map/all_to_all | solution.py:72
  59.5 1.9 %collective-permute-start.8 = (bf16[2,4,16,512]{3,2,1,0:T(8,128)(2,1)S(1)}, bf16[2,4,16,512]{3,2,1,0:T(8,128)(2,1)S(1)}, u32[]{:S(2)}, u32[]{:S(2)}) collective-permute-start(bf16[2,4,16,512]{3,2,1,0:T(8,128)(2,1)S(1)} %pad_maximum_fusion.1), channel_id=1, source_target_pairs={{0,4},{1,5},{2,6},{3,7},{4,8},{5,9},{6,10},{7,11},{8,12},{9,13},{1... | collective-permute-start | bytes 393224 | tf_op jit(solution)/shard_map/ppermute | solution.py:23
  61.4 5.5 %collective-permute-start.9 = (bf16[2,4,16,512]{3,2,1,0:T(8,128)(2,1)S(1)}, bf16[2,4,16,512]{3,2,1,0:T(8,128)(2,1)S(1)}, u32[]{:S(2)}, u32[]{:S(2)}) collective-permute-start(bf16[2,4,16,512]{3,2,1,0:T(8,128)(2,1)S(1)} %pad_maximum_fusion.1), channel_id=1, source_target_pairs={{0,28},{1,29},{2,30},{3,31},{4,0},{5,1},{6,2},{7,3},{8,4},{9,5},{1... | collective-permute-start | bytes 393224 | tf_op jit(solution)/shard_map/ppermute | solution.py:23
  66.9 0.0 collective-permute-done.6
  66.9 0.0 copy-start
  66.9 0.0 collective-permute-done.7
  67.0 2.0 %collective-permute-done.8 = bf16[2,4,16,512]{3,2,1,0:T(8,128)(2,1)S(1)} collective-permute-done((bf16[2,4,16,512]{3,2,1,0:T(8,128)(2,1)S(1)}, bf16[2,4,16,512]{3,2,1,0:T(8,128)(2,1)S(1)}, u32[]{:S(2)}, u32[]{:S(2)}) %collective-permute-start.8) | collective-permute-done | bytes 131104 | tf_op jit(solution)/shard_map/ppermute | solution.py:23
  69.0 3.0 %collective-permute-done.9 = bf16[2,4,16,512]{3,2,1,0:T(8,128)(2,1)S(1)} collective-permute-done((bf16[2,4,16,512]{3,2,1,0:T(8,128)(2,1)S(1)}, bf16[2,4,16,512]{3,2,1,0:T(8,128)(2,1)S(1)}, u32[]{:S(2)}, u32[]{:S(2)}) %collective-permute-start.9) | collective-permute-done | bytes 131104 | tf_op jit(solution)/shard_map/ppermute | solution.py:23
  72.0 0.0 copy-start.3
  72.0 0.0 copy-start.4
  72.0 2.4 %collective-permute-start.10 = (bf16[12,4,16,512]{3,2,1,0:T(8,128)(2,1)S(1)}, bf16[12,4,16,512]{3,2,1,0:T(8,128)(2,1)S(1)}, u32[]{:S(2)}, u32[]{:S(2)}) collective-permute-start(bf16[12,4,16,512]{3,2,1,0:T(8,128)(2,1)S(1)} %constant_dynamic-update-slice_fusion.refs_2_), channel_id=1, source_target_pairs={{0,1},{1,0},{2,3},{3,2},{4,5},{5,4},{6,7},{7,6},{8,9},{9,8},{10,11... | collective-permute-start | bytes 2359304 | tf_op jit(solution)/shard_map/ppermute | solution.py:27
  74.4 1.9 %collective-permute-start.5 = (bf16[4,4,16,512]{3,2,1,0:T(8,128)(2,1)S(1)}, bf16[4,4,16,512]{3,2,1,0:T(8,128)(2,1)S(1)}, u32[]{:S(2)}, u32[]{:S(2)}) collective-permute-start(bf16[4,4,16,512]{3,2,1,0:T(8,128)(2,1)S(1)} %pad_maximum_fusion.refs_0_), channel_id=1, source_target_pairs={{0,1},{1,0},{2,3},{3,2},{4,5},{5,4},{6,7},{7,6},{8,9},{9,8},{10,11... | collective-permute-start | bytes 786440 | tf_op jit(solution)/shard_map/ppermute | solution.py:27
  77.0 0.8 %collective-permute-done.5.refs_1_ = bf16[4,4,16,512]{3,2,1,0:T(8,128)(2,1)S(1)} collective-permute-done((bf16[4,4,16,512]{3,2,1,0:T(8,128)(2,1)S(1)}, bf16[4,4,16,512]{3,2,1,0:T(8,128)(2,1)S(1)}, u32[]{:S(2)}, u32[]{:S(2)}) %collective-permute-start.5) | collective-permute-done | bytes 262176 | tf_op jit(solution)/shard_map/ppermute | solution.py:27
  77.8 0.0 copy-start.1
  77.8 0.7 copy-done.1
  78.5 0.0 all-to-all-done.right_ref
  78.5 0.0 collective-permute-done.10.refs_3_
  78.5 0.0 copy-done
  78.5 0.0 copy-done.3
  78.6 0.0 copy-done.4
  78.6 0.0 copy-start.2
  78.6 0.9 %copy-done.2 = bf16[4,4,16,512]{3,2,1,0:T(8,128)(2,1)S(1)} copy-done((bf16[4,4,16,512]{3,2,1,0:T(8,128)(2,1)S(1)}, bf16[4,4,16,512]{3,2,1,0:T(8,128)(2,1)}, u32[]{:S(2)}) %copy-start.2) | copy-done | bytes 262168
  79.5 3.7 %shard_map.55 = bf16[2,512,512]{2,1,0:T(8,128)(2,1)} custom-call(s32[1,1,2]{2,1,0:T(1,128)S(1)} %copy-done.3, s32[1,1,2]{2,1,0:T(1,128)S(1)} %copy-done.4, s32[1,1]{1,0:T(1,128)S(6)} %copy.9.live_ref, bf16[512,512]{1,0:T(8,128)(2,1)S(1)} %copy-done, bf16[16,2,2,16,512]{4,3,2,1,0:T(8,128)(2,1)S(1)} %all-to-all-done.right_ref, ...), custom_call_target="tpu_custom_call" | custom-call | tf_op jit(solution)/shard_map/pallas_call | solution.py:118
  (9 shorter events, 0.1 us)
Async XLA Ops:
  0.0 25.6 %copy-start.5 = (bf16[4,1,16,512]{3,2,1,0:T(8,128)(2,1)S(1)}, bf16[4,1,16,512]{3,2,1,0:T(8,128)(2,1)}, u32[]{:S(2)}) copy-start(bf16[4,1,16,512]{3,2,1,0:T(8,128)(2,1)} %param.5) | copy-start | bytes 196612
  0.0 35.7 %collective-permute-start.4 = (bf16[1,4,16,512]{3,2,1,0:T(8,128)(2,1)}, bf16[1,4,16,512]{3,2,1,0:T(8,128)(2,1)S(1)}, u32[]{:S(2)}, u32[]{:S(2)}) collective-permute-start(bf16[1,4,16,512]{3,2,1,0:T(8,128)(2,1)} %bitcast.11), channel_id=1, source_target_pairs={{0,16},{1,17},{2,18},{3,19},{4,20},{5,21},{6,22},{7,23},{8,24},{9,... | collective-permute-start | bytes 196616 | tf_op jit(solution)/shard_map/ppermute | solution.py:23
  16.4 19.3 %collective-permute-start.2 = (bf16[1,4,16,512]{3,2,1,0:T(8,128)(2,1)}, bf16[1,4,16,512]{3,2,1,0:T(8,128)(2,1)S(1)}, u32[]{:S(2)}, u32[]{:S(2)}) collective-permute-start(bf16[1,4,16,512]{3,2,1,0:T(8,128)(2,1)} %bitcast.12), channel_id=1, source_target_pairs={{0,8},{1,9},{2,10},{3,11},{4,12},{5,13},{6,14},{7,15},{8,16},{9,17... | collective-permute-start | bytes 196616 | tf_op jit(solution)/shard_map/ppermute | solution.py:23
  20.4 15.3 %collective-permute-start.3 = (bf16[1,4,16,512]{3,2,1,0:T(8,128)(2,1)}, bf16[1,4,16,512]{3,2,1,0:T(8,128)(2,1)S(1)}, u32[]{:S(2)}, u32[]{:S(2)}) collective-permute-start(bf16[1,4,16,512]{3,2,1,0:T(8,128)(2,1)} %bitcast.13), channel_id=1, source_target_pairs={{0,24},{1,25},{2,26},{3,27},{4,28},{5,29},{6,30},{7,31},{8,0},{9,1... | collective-permute-start | bytes 196616 | tf_op jit(solution)/shard_map/ppermute | solution.py:23
  25.7 12.1 %collective-permute-start = (bf16[2,16,512]{2,1,0:T(8,128)(2,1)S(1)}, bf16[2,16,512]{2,1,0:T(8,128)(2,1)S(1)}, u32[]{:S(2)}, u32[]{:S(2)}) collective-permute-start(bf16[2,16,512]{2,1,0:T(8,128)(2,1)S(1)} %get-tuple-element.7), channel_id=1, source_target_pairs={{0,16},{1,0},{2,48},{3,32},{4,80},{5,64},{6,112},{7,96},{8,144},{9... | collective-permute-start | bytes 98312 | tf_op jit(solution)/shard_map/ppermute | solution.py:66
  29.1 8.6 %collective-permute-start.1 = (bf16[2,16,512]{2,1,0:T(8,128)(2,1)S(1)}, bf16[2,16,512]{2,1,0:T(8,128)(2,1)S(1)}, u32[]{:S(2)}, u32[]{:S(2)}) collective-permute-start(bf16[2,16,512]{2,1,0:T(8,128)(2,1)S(1)} %get-tuple-element.8), channel_id=1, source_target_pairs={{0,0},{1,16},{2,32},{3,48},{4,64},{5,80},{6,96},{7,112},{8,128},{9... | collective-permute-start | bytes 98312 | tf_op jit(solution)/shard_map/ppermute | solution.py:66
  35.7 31.2 %collective-permute-start.6 = (bf16[4,4,16,512]{3,2,1,0:T(8,128)(2,1)S(1)}, bf16[4,4,16,512]{3,2,1,0:T(8,128)(2,1)S(1)}, u32[]{:S(2)}, u32[]{:S(2)}) collective-permute-start(bf16[4,4,16,512]{3,2,1,0:T(8,128)(2,1)S(1)} %pad_maximum_fusion.refs_0_), channel_id=1, source_target_pairs={{0,2},{1,3},{2,4},{3,5},{4,6},{5,7},{6,8},{7,9},{8,10},{9,11},{10,... | collective-permute-start | bytes 786440 | tf_op jit(solution)/shard_map/ppermute | solution.py:23
  37.8 29.2 %collective-permute-start.7 = (bf16[4,4,16,512]{3,2,1,0:T(8,128)(2,1)S(1)}, bf16[4,4,16,512]{3,2,1,0:T(8,128)(2,1)S(1)}, u32[]{:S(2)}, u32[]{:S(2)}) collective-permute-start(bf16[4,4,16,512]{3,2,1,0:T(8,128)(2,1)S(1)} %pad_maximum_fusion.refs_0_), channel_id=1, source_target_pairs={{0,30},{1,31},{2,0},{3,1},{4,2},{5,3},{6,4},{7,5},{8,6},{9,7},{10,... | collective-permute-start | bytes 786440 | tf_op jit(solution)/shard_map/ppermute | solution.py:23
  50.1 28.5 %all-to-all-start = ((bf16[16,2,2,16,512]{4,3,2,1,0:T(8,128)(2,1)}), bf16[16,2,2,16,512]{4,3,2,1,0:T(8,128)(2,1)S(1)}, u32[]{:S(2)}, u32[]{:S(2)}) async-start(bf16[16,2,2,16,512]{4,3,2,1,0:T(8,128)(2,1)} %broadcast_in_dim.4), calls=%async_computation | async-start | bytes 2097152 | tf_op jit(solution)/shard_map/all_to_all | solution.py:72
  59.5 9.5 %collective-permute-start.8 = (bf16[2,4,16,512]{3,2,1,0:T(8,128)(2,1)S(1)}, bf16[2,4,16,512]{3,2,1,0:T(8,128)(2,1)S(1)}, u32[]{:S(2)}, u32[]{:S(2)}) collective-permute-start(bf16[2,4,16,512]{3,2,1,0:T(8,128)(2,1)S(1)} %pad_maximum_fusion.1), channel_id=1, source_target_pairs={{0,4},{1,5},{2,6},{3,7},{4,8},{5,9},{6,10},{7,11},{8,12},{9,13},{1... | collective-permute-start | bytes 393224 | tf_op jit(solution)/shard_map/ppermute | solution.py:23
  61.4 10.6 %collective-permute-start.9 = (bf16[2,4,16,512]{3,2,1,0:T(8,128)(2,1)S(1)}, bf16[2,4,16,512]{3,2,1,0:T(8,128)(2,1)S(1)}, u32[]{:S(2)}, u32[]{:S(2)}) collective-permute-start(bf16[2,4,16,512]{3,2,1,0:T(8,128)(2,1)S(1)} %pad_maximum_fusion.1), channel_id=1, source_target_pairs={{0,28},{1,29},{2,30},{3,31},{4,0},{5,1},{6,2},{7,3},{8,4},{9,5},{1... | collective-permute-start | bytes 393224 | tf_op jit(solution)/shard_map/ppermute | solution.py:23
  66.9 11.6 %copy-start = (bf16[512,512]{1,0:T(8,128)(2,1)S(1)}, bf16[512,512]{1,0:T(8,128)(2,1)}, u32[]{:S(2)}) copy-start(bf16[512,512]{1,0:T(8,128)(2,1)} %w_ref.1) | copy-start | bytes 1572868
  72.0 6.6 %copy-start.3 = (s32[1,1,2]{2,1,0:T(1,128)S(1)}, s32[1,1,2]{2,1,0:T(1,128)}, u32[]{:S(2)}) copy-start(s32[1,1,2]{2,1,0:T(1,128)} %rows_ref.1) | copy-start | bytes 28
  72.0 6.6 %copy-start.4 = (s32[1,1,2]{2,1,0:T(1,128)S(1)}, s32[1,1,2]{2,1,0:T(1,128)}, u32[]{:S(2)}) copy-start(s32[1,1,2]{2,1,0:T(1,128)} %cols_ref.1) | copy-start | bytes 28
  72.0 6.5 %collective-permute-start.10 = (bf16[12,4,16,512]{3,2,1,0:T(8,128)(2,1)S(1)}, bf16[12,4,16,512]{3,2,1,0:T(8,128)(2,1)S(1)}, u32[]{:S(2)}, u32[]{:S(2)}) collective-permute-start(bf16[12,4,16,512]{3,2,1,0:T(8,128)(2,1)S(1)} %constant_dynamic-update-slice_fusion.refs_2_), channel_id=1, source_target_pairs={{0,1},{1,0},{2,3},{3,2},{4,5},{5,4},{6,7},{7,6},{8,9},{9,8},{10,11... | collective-permute-start | bytes 2359304 | tf_op jit(solution)/shard_map/ppermute | solution.py:27
  74.4 3.4 %collective-permute-start.5 = (bf16[4,4,16,512]{3,2,1,0:T(8,128)(2,1)S(1)}, bf16[4,4,16,512]{3,2,1,0:T(8,128)(2,1)S(1)}, u32[]{:S(2)}, u32[]{:S(2)}) collective-permute-start(bf16[4,4,16,512]{3,2,1,0:T(8,128)(2,1)S(1)} %pad_maximum_fusion.refs_0_), channel_id=1, source_target_pairs={{0,1},{1,0},{2,3},{3,2},{4,5},{5,4},{6,7},{7,6},{8,9},{9,8},{10,11... | collective-permute-start | bytes 786440 | tf_op jit(solution)/shard_map/ppermute | solution.py:27
  77.8 0.7 copy-start.1
  78.6 1.0 %copy-start.2 = (bf16[4,4,16,512]{3,2,1,0:T(8,128)(2,1)S(1)}, bf16[4,4,16,512]{3,2,1,0:T(8,128)(2,1)}, u32[]{:S(2)}) copy-start(bf16[4,4,16,512]{3,2,1,0:T(8,128)(2,1)} %copy-done.1) | copy-start | bytes 786436

commit v2 on v0

v2 whole, which is shorter than its diff:
```python
import functools

import jax
import jax.numpy as jnp
from jax import lax
from jax.experimental import pallas as pl
from jax.experimental.pallas import tpu as pltpu
from jax.sharding import PartitionSpec as P

CHIPS = 16
COLS = 2 * CHIPS
ROWS = 16
SIDE = 4


def swap_core(value):
    return lax.ppermute(value, "col", [(i, i ^ 1) for i in range(COLS)])


def spread_z(value, hops):
    return lax.ppermute(
        value, "col", [(i, (i + (2 * hops if i % 2 == 0 else -2 * hops)) % COLS) for i in range(COLS)]
    )


def ring(delta, size):
    return min(delta % size, -delta % size)


def relay_steps():
    along = sorted(range(CHIPS), key=lambda d: -ring(d, CHIPS))
    across = sorted(range(ROWS), key=lambda s: ring(s // SIDE, SIDE) + ring(s % SIDE, SIDE))
    steps = dict(zip(along, across))
    return [(steps[d] // SIDE, steps[d] % SIDE) for d in range(CHIPS)]


def relay_row(row, step):
    return (row // SIDE + step[0]) % SIDE * SIDE + (row + step[1]) % SIDE


def scatter(value):
    steps = relay_steps()
    perm = []
    for r in range(ROWS):
        for c in range(COLS):
            target = r + ROWS * (c % 2)
            step = steps[(c // 2 - target // 2) % CHIPS]
            perm.append((r * COLS + c, relay_row(r, step) * COLS + target))
    return lax.ppermute(value, ("row", "col"), perm)


def update_kernel(plan, rows_ref, cols_ref, live_ref, w_ref, right_ref, *refs):
    lefts, (out_ref, a_ref, f_ref) = refs[:-3], refs[-3:]
    col = lax.axis_index("col")
    z = lax.div(col, 2)
    core = lax.rem(col, 2)
    high = lax.div(col, ROWS)
    root = lax.rem(col, ROWS)
    live = live_ref[0, 0]
    w = w_ref[...]
    dims = (((1,), (1,)), ((), ()))

    def place(origin, part, tile):
        start = pl.multiple_of((2 * lax.rem(origin + 2 * CHIPS, CHIPS) + part) * 16, 16)
        a_ref[pl.ds(start, 16), :] = tile

    for b in range(2):
        for delta, step in enumerate(relay_steps()):
            row = lax.rem(lax.div(root, SIDE) + step[0], SIDE) * SIDE + lax.rem(root + step[1], SIDE)
            for part in range(2):
                place(z + delta, lax.rem(high + part, 2), right_ref[row, part, b])
        f_ref[b] = jnp.dot(a_ref[...], w, preferred_element_type=jnp.float32).astype(jnp.bfloat16)
    for slot in range(2):

        @pl.when(slot < live)
        def _():
            a = rows_ref[0, 0, slot] // ROWS
            b = cols_ref[0, 0, slot] // COLS
            for which, first, hops, swapped in plan:
                way, base = (1 - 2 * core, 1 - core) if swapped else (2 * core - 1, core)
                for index, (hop, part) in enumerate(hops):
                    place(z + way * hop, lax.rem(base + part, 2), lefts[which][first + index, a])
            left = jnp.dot(a_ref[...], w, preferred_element_type=jnp.float32).astype(jnp.bfloat16)
            product = lax.dot_general(left, f_ref[b], dims, preferred_element_type=jnp.float32)
            out_ref[slot] = (-product).astype(jnp.bfloat16)

        @pl.when(slot >= live)
        def _():
            out_ref[slot] = jnp.zeros_like(out_ref[slot])


def pairs(*hops):
    return tuple((hop, part) for hop in hops for part in range(2))


def body(panel, inverse_factor, slot_rows, slot_cols, live_count):
    piece = panel[:, 0]
    size = inverse_factor.shape[0]
    core = lax.axis_index("col") % 2

    other = swap_core(piece)
    pair = jnp.stack([piece, other])
    g4 = spread_z(pair, 4)
    mine = jnp.stack(
        [
            lax.dynamic_index_in_dim(part.reshape(2, 2, *piece.shape[1:]), core, 1, keepdims=False)
            for part in (piece, other)
        ]
    )
    scattered, g4 = lax.optimization_barrier((scatter(mine), g4))
    fanned = jnp.broadcast_to(scattered[None], (ROWS, *scattered.shape))
    right = lax.all_to_all(fanned, "row", 0, 0, tiled=True)

    near = jnp.concatenate([pair, g4])
    g2 = spread_z(near, 2)
    g1a = spread_z(near, 1)
    g1b = spread_z(g2, 1)
    edge = spread_z(g2[2:], 2)
    early = jnp.concatenate([g4, g2, g1a])
    early2 = swap_core(early)
    g1b, edge, right, early2 = lax.optimization_barrier((g1b, edge, right, early2))
    lefts = [pair, early, g1b, edge, early2, swap_core(g1b)]
    hops = pairs(4, 2, 6, 1, 5)
    plan = (
        (0, 0, pairs(0), False),
        (1, 0, hops, False),
        (2, 0, pairs(3, 7), False),
        (3, 0, pairs(8), False),
        (4, 0, hops, True),
        (5, 0, pairs(3, 7), True),
    )

    smem = pl.BlockSpec(memory_space=pltpu.SMEM)
    vmem = pl.BlockSpec(memory_space=pltpu.VMEM)
    out = pl.pallas_call(
        functools.partial(update_kernel, plan),
        out_shape=jax.ShapeDtypeStruct((2, size, size), jnp.bfloat16),
        in_specs=[smem] * 3 + [vmem] * (2 + len(lefts)),
        out_specs=vmem,
        scratch_shapes=[
            pltpu.VMEM((size, size), jnp.bfloat16),
            pltpu.VMEM((2, size, size), jnp.bfloat16),
        ],
        compiler_params=pltpu.CompilerParams(vmem_limit_bytes=16 * 2**20),
    )(slot_rows, slot_cols, live_count, inverse_factor, right, *lefts)
    return out[None, None]


def solution(mesh):
    placed = (
        P(None, "row", "col", None),
        P(),
        P("row", "col", None),
        P("row", "col", None),
        P("row", "col"),
    )
    return jax.shard_map(
        body,
        mesh=mesh,
        in_specs=placed,
        out_specs=P("row", "col", None, None, None),
        check_vma=False,
    )
```

time: 230 us -> 72.8 us (0.32)
  the two profiles are of different devices: /device:TPU:2 before, /device:TPU:1 now
where the time goes in v2:
time: 72.8 us; the launch traced here: 72.3 us
  starting transfers between devices  48.6 us (67%)
  waiting for transfers between devices  15.1 us (21%)
  Pallas kernels  3.89 us (5%)
  local copies, waits for them, and re-layouts  3.87 us (5%)
  between operations  0.83 us (1%)
    ppermute x5, starting transfers between devices, spread_z(): lax.ppermute(value, 'col', [(i, (i + (2 * hops if i % 2 == 0 else -2 * ho...  21.7 us
    ppermute x3, starting transfers between devices, swap_core(): return lax.ppermute(value, 'col', [(i, i ^ 1) for i in range(COLS)])  14.7 us
    ppermute x1, starting transfers between devices, scatter(): return lax.ppermute(value, ('row', 'col'), perm)  7.52 us
    ppermute x1, waiting for transfers between devices, scatter(): return lax.ppermute(value, ('row', 'col'), perm)  7.08 us
    ppermute x5, waiting for transfers between devices, spread_z(): lax.ppermute(value, 'col', [(i, (i + (2 * hops if i % 2 == 0 else -2 * ho...  6.42 us
    all_to_all x1, starting transfers between devices, body(): right = lax.all_to_all(fanned, 'row', 0, 0, tiled=True)  4.62 us
    pallas_call x1, Pallas kernels, body(): pl.pallas_call(functools.partial(update_kernel, plan), out_shape=jax.Shap...  3.89 us
  transfers between devices with their start and end apart: 10, of which 5 were waited for; matrix products, arithmetic and copies ran while one was open for 5% of the time, Pallas kernels for 0%

profile of v2, /device:TPU:1, one launch (start us, length us, event | category | flops | bytes accessed | tf_op | source)
XLA Modules:
  0.0 72.3 jit_solution(2559995456138489642)
XLA Ops:
  0.0 8.8 %collective-permute-start = (bf16[4,16,512]{2,1,0:T(8,128)(2,1)}, bf16[4,16,512]{2,1,0:T(8,128)(2,1)S(1)}, u32[]{:S(2)}, u32[]{:S(2)}) collective-permute-start(bf16[4,16,512]{2,1,0:T(8,128)(2,1)} %bitcast.10), channel_id=1, source_target_pairs={{0,1},{1,0},{2,3},{3,2},{4,5},{5,4},{6,7},{7,6},{8,9},{9,8},{10,11... | collective-permute-start | bytes 196616 | tf_op jit(solution)/shard_map/ppermute | solution.py:17
  8.8 0.0 copy-start.3
  8.8 0.8 %dynamic-slice_bitcast_fusion.1 = bf16[1,2,16,512]{3,2,1,0:T(8,128)(2,1)S(1)} fusion(bf16[2,2,16,512]{3,2,1,0:T(8,128)(2,1)} %bitcast.11, s32[]{:T(128)S(6)} %select_n.13), kind=kLoop, calls=%fused_computation.4 | loop fusion | bytes 65540 | tf_op jit(solution)/shard_map/stack | solution.py:104
  9.6 0.2 collective-permute-done
  9.9 0.0 copy-done.3
  9.9 7.1 %collective-permute-start.2 = (bf16[2,4,16,512]{3,2,1,0:T(8,128)(2,1)S(1)}, bf16[2,4,16,512]{3,2,1,0:T(8,128)(2,1)S(1)}, u32[]{:S(2)}, u32[]{:S(2)}) collective-permute-start(bf16[2,4,16,512]{3,2,1,0:T(8,128)(2,1)S(1)} %pad_maximum_fusion.1.refs_0_), channel_id=1, source_target_pairs={{0,8},{1,25},{2,10},{3,27},{4,12},{5,29},{6,14},{7,31},{8,16},{9,1... | collective-permute-start | bytes 393224 | tf_op jit(solution)/shard_map/ppermute | solution.py:21
  17.0 7.5 %collective-permute-start.1 = (bf16[2,2,16,512]{3,2,1,0:T(8,128)(2,1)S(1)}, bf16[2,2,16,512]{3,2,1,0:T(8,128)(2,1)S(1)}, u32[]{:S(2)}, u32[]{:S(2)}) collective-permute-start(bf16[2,2,16,512]{3,2,1,0:T(8,128)(2,1)S(1)} %pad_maximum_fusion.2), channel_id=1, source_target_pairs={{0,320},{1,16},{2,352},{3,112},{4,192},{5,400},{6,416},{7,176},{8,... | collective-permute-start | bytes 196616 | tf_op jit(solution)/shard_map/ppermute | solution.py:49
  24.5 7.1 %collective-permute-done.1 = bf16[2,2,16,512]{3,2,1,0:T(8,128)(2,1)S(1)} collective-permute-done((bf16[2,2,16,512]{3,2,1,0:T(8,128)(2,1)S(1)}, bf16[2,2,16,512]{3,2,1,0:T(8,128)(2,1)S(1)}, u32[]{:S(2)}, u32[]{:S(2)}) %collective-permute-start.1) | collective-permute-done | bytes 65568 | tf_op jit(solution)/shard_map/ppermute | solution.py:49
  31.6 0.0 collective-permute-done.2
  31.6 1.9 %collective-permute-start.3 = (bf16[4,4,16,512]{3,2,1,0:T(8,128)(2,1)S(1)}, bf16[4,4,16,512]{3,2,1,0:T(8,128)(2,1)}, u32[]{:S(2)}, u32[]{:S(2)}) collective-permute-start(bf16[4,4,16,512]{3,2,1,0:T(8,128)(2,1)S(1)} %pad_maximum_fusion), channel_id=1, source_target_pairs={{0,4},{1,29},{2,6},{3,31},{4,8},{5,1},{6,10},{7,3},{8,12},{9,5},{1... | collective-permute-start | bytes 786440 | tf_op jit(solution)/shard_map/ppermute | solution.py:21
  33.6 7.3 %collective-permute-start.6 = (bf16[4,4,16,512]{3,2,1,0:T(8,128)(2,1)S(1)}, bf16[4,4,16,512]{3,2,1,0:T(8,128)(2,1)S(1)}, u32[]{:S(2)}, u32[]{:S(2)}) collective-permute-start(bf16[4,4,16,512]{3,2,1,0:T(8,128)(2,1)S(1)} %pad_maximum_fusion), channel_id=1, source_target_pairs={{0,2},{1,31},{2,4},{3,1},{4,6},{5,3},{6,8},{7,5},{8,10},{9,7},{10,... | collective-permute-start | bytes 786440 | tf_op jit(solution)/shard_map/ppermute | solution.py:21
  40.8 1.1 %broadcast_in_dim.4 = bf16[16,2,2,16,512]{4,3,2,1,0:T(8,128)(2,1)} broadcast(bf16[2,2,16,512]{3,2,1,0:T(8,128)(2,1)S(1)} %collective-permute-done.1), dimensions={1,2,3,4} | broadcast | bytes 1114112 | tf_op jit(solution)/shard_map/broadcast_in_dim | solution.py:111
  41.9 4.6 %all-to-all-start = ((bf16[16,2,2,16,512]{4,3,2,1,0:T(8,128)(2,1)}), bf16[16,2,2,16,512]{4,3,2,1,0:T(8,128)(2,1)S(1)}, u32[]{:S(2)}, u32[]{:S(2)}) async-start(bf16[16,2,2,16,512]{4,3,2,1,0:T(8,128)(2,1)} %broadcast_in_dim.4), calls=%async_computation | async-start | bytes 2097152 | tf_op jit(solution)/shard_map/all_to_all | solution.py:112
  46.6 0.0 collective-permute-done.3
  46.6 1.0 %constant_dynamic-update-slice_fusion.1 = bf16[10,4,16,512]{3,2,1,0:T(8,128)(2,1)S(1)} fusion(bf16[10,4,16,512]{3,2,1,0:T(8,128)(2,1)S(1)} %constant_dynamic-update-slice_fusion.2, bf16[4,4,16,512]{3,2,1,0:T(8,128)(2,1)} %collective-permute-done.3), kind=kLoop, calls=%fused_computation.6 | loop fusion | bytes 524288
  47.6 0.0 copy-start
  47.6 0.0 collective-permute-done.6
  47.6 2.4 %collective-permute-start.7 = (bf16[10,4,16,512]{3,2,1,0:T(8,128)(2,1)S(1)}, bf16[10,4,16,512]{3,2,1,0:T(8,128)(2,1)S(1)}, u32[]{:S(2)}, u32[]{:S(2)}) collective-permute-start(bf16[10,4,16,512]{3,2,1,0:T(8,128)(2,1)S(1)} %constant_dynamic-update-slice_fusion.refs_1_), channel_id=1, source_target_pairs={{0,1},{1,0},{2,3},{3,2},{4,5},{5,4},{6,7},{7,6},{8,9},{9,8},{10,11... | collective-permute-start | bytes 1966088 | tf_op jit(solution)/shard_map/ppermute | solution.py:17
  50.0 2.1 %collective-permute-start.4 = (bf16[4,4,16,512]{3,2,1,0:T(8,128)(2,1)}, bf16[4,4,16,512]{3,2,1,0:T(8,128)(2,1)S(1)}, u32[]{:S(2)}, u32[]{:S(2)}) collective-permute-start(bf16[4,4,16,512]{3,2,1,0:T(8,128)(2,1)} %collective-permute-done.3), channel_id=1, source_target_pairs={{0,2},{1,31},{2,4},{3,1},{4,6},{5,3},{6,8},{7,5},{8,10},{9,7},{10,... | collective-permute-start | bytes 786440 | tf_op jit(solution)/shard_map/ppermute | solution.py:21
  52.2 0.9 %slice.4 = bf16[2,4,16,512]{3,2,1,0:T(8,128)(2,1)S(1)} slice(bf16[4,4,16,512]{3,2,1,0:T(8,128)(2,1)} %collective-permute-done.3), slice={[2:4], [0:4], [0:16], [0:512]} | slice | bytes 262144 | tf_op jit(solution)/shard_map/slice | solution.py:118
  53.1 0.0 copy-start.1
  53.1 0.0 copy-start.2
  53.1 3.4 %collective-permute-start.5 = (bf16[2,4,16,512]{3,2,1,0:T(8,128)(2,1)S(1)}, bf16[2,4,16,512]{3,2,1,0:T(8,128)(2,1)S(1)}, u32[]{:S(2)}, u32[]{:S(2)}) collective-permute-start(bf16[2,4,16,512]{3,2,1,0:T(8,128)(2,1)S(1)} %slice.4), channel_id=1, source_target_pairs={{0,4},{1,29},{2,6},{3,31},{4,8},{5,1},{6,10},{7,3},{8,12},{9,5},{1... | collective-permute-start | bytes 393224 | tf_op jit(solution)/shard_map/ppermute | solution.py:21
  56.5 6.4 %collective-permute-done.5.refs_3_ = bf16[2,4,16,512]{3,2,1,0:T(8,128)(2,1)S(1)} collective-permute-done((bf16[2,4,16,512]{3,2,1,0:T(8,128)(2,1)S(1)}, bf16[2,4,16,512]{3,2,1,0:T(8,128)(2,1)S(1)}, u32[]{:S(2)}, u32[]{:S(2)}) %collective-permute-start.5) | collective-permute-done | bytes 131104 | tf_op jit(solution)/shard_map/ppermute | solution.py:21
  62.9 0.0 collective-permute-done.4.refs_2_
  62.9 0.0 collective-permute-done.7.refs_4_
  62.9 0.8 %all-to-all-done.right_ref = bf16[16,2,2,16,512]{4,3,2,1,0:T(8,128)(2,1)S(1)} async-done(((bf16[16,2,2,16,512]{4,3,2,1,0:T(8,128)(2,1)}), bf16[16,2,2,16,512]{4,3,2,1,0:T(8,128)(2,1)S(1)}, u32[]{:S(2)}, u32[]{:S(2)}) %all-to-all-start) | async-done | bytes 1048608 | tf_op jit(solution)/shard_map/all_to_all | solution.py:112
  63.7 3.5 %collective-permute-start.8 = (bf16[4,4,16,512]{3,2,1,0:T(8,128)(2,1)S(1)}, bf16[4,4,16,512]{3,2,1,0:T(8,128)(2,1)S(1)}, u32[]{:S(2)}, u32[]{:S(2)}) collective-permute-start(bf16[4,4,16,512]{3,2,1,0:T(8,128)(2,1)S(1)} %collective-permute-done.4.refs_2_), channel_id=1, source_target_pairs={{0,1},{1,0},{2,3},{3,2},{4,5},{5,4},{6,7},{7,6},{8,9},{9,8},{10,11... | collective-permute-start | bytes 786440 | tf_op jit(solution)/shard_map/ppermute | solution.py:17
  67.9 0.5 collective-permute-done.8.refs_5_
  68.4 0.0 copy-done
  68.4 0.0 copy-done.1
  68.4 0.0 copy-done.2
  68.4 3.9 %shard_map.55 = bf16[2,512,512]{2,1,0:T(8,128)(2,1)} custom-call(s32[1,1,2]{2,1,0:T(1,128)S(1)} %copy-done.1, s32[1,1,2]{2,1,0:T(1,128)S(1)} %copy-done.2, s32[1,1]{1,0:T(1,128)S(6)} %copy.8.live_ref, bf16[512,512]{1,0:T(8,128)(2,1)S(1)} %copy-done, bf16[16,2,2,16,512]{4,3,2,1,0:T(8,128)(2,1)S(1)} %all-to-all-done.right_ref, ...), custom_call_target="tpu_custom_call" | custom-call | tf_op jit(solution)/shard_map/pallas_call | solution.py:135
  (6 shorter events, 0.1 us)
Async XLA Ops:
  0.0 9.9 %collective-permute-start = (bf16[4,16,512]{2,1,0:T(8,128)(2,1)}, bf16[4,16,512]{2,1,0:T(8,128)(2,1)S(1)}, u32[]{:S(2)}, u32[]{:S(2)}) collective-permute-start(bf16[4,16,512]{2,1,0:T(8,128)(2,1)} %bitcast.10), channel_id=1, source_target_pairs={{0,1},{1,0},{2,3},{3,2},{4,5},{5,4},{6,7},{7,6},{8,9},{9,8},{10,11... | collective-permute-start | bytes 196616 | tf_op jit(solution)/shard_map/ppermute | solution.py:17
  8.8 1.1 %copy-start.3 = (bf16[4,1,16,512]{3,2,1,0:T(8,128)(2,1)S(1)}, bf16[4,1,16,512]{3,2,1,0:T(8,128)(2,1)}, u32[]{:S(2)}) copy-start(bf16[4,1,16,512]{3,2,1,0:T(8,128)(2,1)} %param.5) | copy-start | bytes 196612
  9.9 21.7 %collective-permute-start.2 = (bf16[2,4,16,512]{3,2,1,0:T(8,128)(2,1)S(1)}, bf16[2,4,16,512]{3,2,1,0:T(8,128)(2,1)S(1)}, u32[]{:S(2)}, u32[]{:S(2)}) collective-permute-start(bf16[2,4,16,512]{3,2,1,0:T(8,128)(2,1)S(1)} %pad_maximum_fusion.1.refs_0_), channel_id=1, source_target_pairs={{0,8},{1,25},{2,10},{3,27},{4,12},{5,29},{6,14},{7,31},{8,16},{9,1... | collective-permute-start | bytes 393224 | tf_op jit(solution)/shard_map/ppermute | solution.py:21
  17.0 14.6 %collective-permute-start.1 = (bf16[2,2,16,512]{3,2,1,0:T(8,128)(2,1)S(1)}, bf16[2,2,16,512]{3,2,1,0:T(8,128)(2,1)S(1)}, u32[]{:S(2)}, u32[]{:S(2)}) collective-permute-start(bf16[2,2,16,512]{3,2,1,0:T(8,128)(2,1)S(1)} %pad_maximum_fusion.2), channel_id=1, source_target_pairs={{0,320},{1,16},{2,352},{3,112},{4,192},{5,400},{6,416},{7,176},{8,... | collective-permute-start | bytes 196616 | tf_op jit(solution)/shard_map/ppermute | solution.py:49
  31.6 14.9 %collective-permute-start.3 = (bf16[4,4,16,512]{3,2,1,0:T(8,128)(2,1)S(1)}, bf16[4,4,16,512]{3,2,1,0:T(8,128)(2,1)}, u32[]{:S(2)}, u32[]{:S(2)}) collective-permute-start(bf16[4,4,16,512]{3,2,1,0:T(8,128)(2,1)S(1)} %pad_maximum_fusion), channel_id=1, source_target_pairs={{0,4},{1,29},{2,6},{3,31},{4,8},{5,1},{6,10},{7,3},{8,12},{9,5},{1... | collective-permute-start | bytes 786440 | tf_op jit(solution)/shard_map/ppermute | solution.py:21
  33.6 14.0 %collective-permute-start.6 = (bf16[4,4,16,512]{3,2,1,0:T(8,128)(2,1)S(1)}, bf16[4,4,16,512]{3,2,1,0:T(8,128)(2,1)S(1)}, u32[]{:S(2)}, u32[]{:S(2)}) collective-permute-start(bf16[4,4,16,512]{3,2,1,0:T(8,128)(2,1)S(1)} %pad_maximum_fusion), channel_id=1, source_target_pairs={{0,2},{1,31},{2,4},{3,1},{4,6},{5,3},{6,8},{7,5},{8,10},{9,7},{10,... | collective-permute-start | bytes 786440 | tf_op jit(solution)/shard_map/ppermute | solution.py:21
  41.9 21.8 %all-to-all-start = ((bf16[16,2,2,16,512]{4,3,2,1,0:T(8,128)(2,1)}), bf16[16,2,2,16,512]{4,3,2,1,0:T(8,128)(2,1)S(1)}, u32[]{:S(2)}, u32[]{:S(2)}) async-start(bf16[16,2,2,16,512]{4,3,2,1,0:T(8,128)(2,1)} %broadcast_in_dim.4), calls=%async_computation | async-start | bytes 2097152 | tf_op jit(solution)/shard_map/all_to_all | solution.py:112
  47.6 20.8 %copy-start = (bf16[512,512]{1,0:T(8,128)(2,1)S(1)}, bf16[512,512]{1,0:T(8,128)(2,1)}, u32[]{:S(2)}) copy-start(bf16[512,512]{1,0:T(8,128)(2,1)} %w_ref.1) | copy-start | bytes 1572868
  47.6 15.3 %collective-permute-start.7 = (bf16[10,4,16,512]{3,2,1,0:T(8,128)(2,1)S(1)}, bf16[10,4,16,512]{3,2,1,0:T(8,128)(2,1)S(1)}, u32[]{:S(2)}, u32[]{:S(2)}) collective-permute-start(bf16[10,4,16,512]{3,2,1,0:T(8,128)(2,1)S(1)} %constant_dynamic-update-slice_fusion.refs_1_), channel_id=1, source_target_pairs={{0,1},{1,0},{2,3},{3,2},{4,5},{5,4},{6,7},{7,6},{8,9},{9,8},{10,11... | collective-permute-start | bytes 1966088 | tf_op jit(solution)/shard_map/ppermute | solution.py:17
  50.0 12.9 %collective-permute-start.4 = (bf16[4,4,16,512]{3,2,1,0:T(8,128)(2,1)}, bf16[4,4,16,512]{3,2,1,0:T(8,128)(2,1)S(1)}, u32[]{:S(2)}, u32[]{:S(2)}) collective-permute-start(bf16[4,4,16,512]{3,2,1,0:T(8,128)(2,1)} %collective-permute-done.3), channel_id=1, source_target_pairs={{0,2},{1,31},{2,4},{3,1},{4,6},{5,3},{6,8},{7,5},{8,10},{9,7},{10,... | collective-permute-start | bytes 786440 | tf_op jit(solution)/shard_map/ppermute | solution.py:21
  53.1 15.3 %copy-start.1 = (s32[1,1,2]{2,1,0:T(1,128)S(1)}, s32[1,1,2]{2,1,0:T(1,128)}, u32[]{:S(2)}) copy-start(s32[1,1,2]{2,1,0:T(1,128)} %rows_ref.1) | copy-start | bytes 28
  53.1 15.3 %copy-start.2 = (s32[1,1,2]{2,1,0:T(1,128)S(1)}, s32[1,1,2]{2,1,0:T(1,128)}, u32[]{:S(2)}) copy-start(s32[1,1,2]{2,1,0:T(1,128)} %cols_ref.1) | copy-start | bytes 28
  53.1 9.8 %collective-permute-start.5 = (bf16[2,4,16,512]{3,2,1,0:T(8,128)(2,1)S(1)}, bf16[2,4,16,512]{3,2,1,0:T(8,128)(2,1)S(1)}, u32[]{:S(2)}, u32[]{:S(2)}) collective-permute-start(bf16[2,4,16,512]{3,2,1,0:T(8,128)(2,1)S(1)} %slice.4), channel_id=1, source_target_pairs={{0,4},{1,29},{2,6},{3,31},{4,8},{5,1},{6,10},{7,3},{8,12},{9,5},{1... | collective-permute-start | bytes 393224 | tf_op jit(solution)/shard_map/ppermute | solution.py:21
  63.7 4.7 %collective-permute-start.8 = (bf16[4,4,16,512]{3,2,1,0:T(8,128)(2,1)S(1)}, bf16[4,4,16,512]{3,2,1,0:T(8,128)(2,1)S(1)}, u32[]{:S(2)}, u32[]{:S(2)}) collective-permute-start(bf16[4,4,16,512]{3,2,1,0:T(8,128)(2,1)S(1)} %collective-permute-done.4.refs_2_), channel_id=1, source_target_pairs={{0,1},{1,0},{2,3},{3,2},{4,5},{5,4},{6,7},{7,6},{8,9},{9,8},{10,11... | collective-permute-start | bytes 786440 | tf_op jit(solution)/shard_map/ppermute | solution.py:17

commit v3 on v2

--- a/solution.py
+++ b/solution.py
@@ -49,27 +49,36 @@
     return lax.ppermute(value, ("row", "col"), perm)
 
 
-def update_kernel(plan, rows_ref, cols_ref, live_ref, w_ref, right_ref, *refs):
-    lefts, (out_ref, a_ref, f_ref) = refs[:-3], refs[-3:]
+def origin_row(origin, part):
+    return pl.multiple_of((2 * lax.rem(origin + 2 * CHIPS, CHIPS) + part) * 16, 16)
+
+
+def solve(value, w):
+    return jnp.dot(value, w, preferred_element_type=jnp.float32).astype(jnp.bfloat16)
+
+
+def right_kernel(w_ref, right_ref, f_ref, block_ref):
     col = lax.axis_index("col")
     z = lax.div(col, 2)
-    core = lax.rem(col, 2)
     high = lax.div(col, ROWS)
     root = lax.rem(col, ROWS)
-    live = live_ref[0, 0]
     w = w_ref[...]
-    dims = (((1,), (1,)), ((), ()))
-
-    def place(origin, part, tile):
-        start = pl.multiple_of((2 * lax.rem(origin + 2 * CHIPS, CHIPS) + part) * 16, 16)
-        a_ref[pl.ds(start, 16), :] = tile
-
     for b in range(2):
         for delta, step in enumerate(relay_steps()):
             row = lax.rem(lax.div(root, SIDE) + step[0], SIDE) * SIDE + lax.rem(root + step[1], SIDE)
             for part in range(2):
-                place(z + delta, lax.rem(high + part, 2), right_ref[row, part, b])
-        f_ref[b] = jnp.dot(a_ref[...], w, preferred_element_type=jnp.float32).astype(jnp.bfloat16)
+                start = origin_row(z + delta, lax.rem(high + part, 2))
+                block_ref[pl.ds(start, 16), :] = right_ref[row, part, b]
+        f_ref[b] = solve(block_ref[...], w)
+
+
+def update_kernel(plan, rows_ref, cols_ref, live_ref, w_ref, f_ref, *refs):
+    lefts, (out_ref, a_ref) = refs[:-2], refs[-2:]
+    col = lax.axis_index("col")
+    z = lax.div(col, 2)
+    core = lax.rem(col, 2)
+    live = live_ref[0, 0]
+    dims = (((1,), (1,)), ((), ()))
     for slot in range(2):
 
         @pl.when(slot < live)
@@ -79,8 +88,9 @@
             for which, first, hops, swapped in plan:
                 way, base = (1 - 2 * core, 1 - core) if swapped else (2 * core - 1, core)
                 for index, (hop, part) in enumerate(hops):
-                    place(z + way * hop, lax.rem(base + part, 2), lefts[which][first + index, a])
-            left = jnp.dot(a_ref[...], w, preferred_element_type=jnp.float32).astype(jnp.bfloat16)
+                    start = origin_row(z + way * hop, lax.rem(base + part, 2))
+                    a_ref[pl.ds(start, 16), :] = lefts[which][first + index, a]
+            left = solve(a_ref[...], w_ref[...])
             product = lax.dot_general(left, f_ref[b], dims, preferred_element_type=jnp.float32)
             out_ref[slot] = (-product).astype(jnp.bfloat16)
 
@@ -112,37 +122,42 @@
     right = lax.all_to_all(fanned, "row", 0, 0, tiled=True)
 
     near = jnp.concatenate([pair, g4])
-    g2 = spread_z(near, 2)
+    g3 = spread_z(near, 3)
     g1a = spread_z(near, 1)
-    g1b = spread_z(g2, 1)
-    edge = spread_z(g2[2:], 2)
-    early = jnp.concatenate([g4, g2, g1a])
-    early2 = swap_core(early)
-    g1b, edge, right, early2 = lax.optimization_barrier((g1b, edge, right, early2))
-    lefts = [pair, early, g1b, edge, early2, swap_core(g1b)]
-    hops = pairs(4, 2, 6, 1, 5)
+    g1b = spread_z(jnp.concatenate([g1a, g3[2:3]]), 1)
+    early = jnp.concatenate([g4, g3, g1a])
+    lefts = [pair, early, g1b, swap_core(early), swap_core(g1b)]
+    hops = pairs(4, 3, 7, 1, 5)
+    last = pairs(2, 6) + ((8, 0),)
     plan = (
         (0, 0, pairs(0), False),
         (1, 0, hops, False),
-        (2, 0, pairs(3, 7), False),
-        (3, 0, pairs(8), False),
-        (4, 0, hops, True),
-        (5, 0, pairs(3, 7), True),
+        (2, 0, last, False),
+        (3, 0, hops, True),
+        (4, 0, last, True),
     )
 
     smem = pl.BlockSpec(memory_space=pltpu.SMEM)
     vmem = pl.BlockSpec(memory_space=pltpu.VMEM)
+    blocks = jax.ShapeDtypeStruct((2, size, size), jnp.bfloat16)
+    params = pltpu.CompilerParams(vmem_limit_bytes=8 * 2**20)
+    solved = pl.pallas_call(
+        right_kernel,
+        out_shape=blocks,
+        in_specs=[vmem] * 2,
+        out_specs=vmem,
+        scratch_shapes=[pltpu.VMEM((size, size), jnp.bfloat16)],
+        cost_estimate=pl.CostEstimate(flops=4 * size**3, bytes_accessed=2**22, transcendentals=0),
+        compiler_params=params,
+    )(inverse_factor, right)
     out = pl.pallas_call(
         functools.partial(update_kernel, plan),
-        out_shape=jax.ShapeDtypeStruct((2, size, size), jnp.bfloat16),
+        out_shape=blocks,
         in_specs=[smem] * 3 + [vmem] * (2 + len(lefts)),
         out_specs=vmem,
-        scratch_shapes=[
-            pltpu.VMEM((size, size), jnp.bfloat16),
-            pltpu.VMEM((2, size, size), jnp.bfloat16),
-        ],
-        compiler_params=pltpu.CompilerParams(vmem_limit_bytes=16 * 2**20),
-    )(slot_rows, slot_cols, live_count, inverse_factor, right, *lefts)
+        scratch_shapes=[pltpu.VMEM((size, size), jnp.bfloat16)],
+        compiler_params=params,
+    )(slot_rows, slot_cols, live_count, inverse_factor, solved, *lefts)
     return out[None, None]
 
 

time: 72.8 us -> 67.7 us (0.930)
  waiting for transfers between devices: 15.1 us -> 11.7 us
  local copies, waits for them, and re-layouts: 3.87 us -> 2.01 us
    ppermute x5 -> x4, waiting for transfers between devices: 6.42 us -> 4.33 us  [spread_z(): lax.ppermute(value, 'col', [(i, (i + (2 * hops if i % 2 == 0 else -2 * ho...]
    unnamed x10, local copies, waits for them, and re-layouts: 1 us -> 0.05 us
    slice x1, local copies, waits for them, and re-layouts: 0.92 us -> 0.01 us  [body(): g1b = spread_z(jnp.concatenate([g1a, g3[2:3]]), 1)]
    all_to_all x1, waiting for transfers between devices: 0.84 us -> 0.01 us  [body(): right = lax.all_to_all(fanned, 'row', 0, 0, tiled=True)]
    ppermute x5 -> x4, starting transfers between devices: 21.7 us -> 21.1 us  [spread_z(): lax.ppermute(value, 'col', [(i, (i + (2 * hops if i % 2 == 0 else -2 * ho...]
    pallas_call x1 -> x2, Pallas kernels: 3.89 us -> 4.34 us  [the longest x1 3.54 us: body(): pl.pallas_call(functools.partial(update_kernel, plan), out_shape=blocks,...]
  transfers between devices with their start and end apart: 10 -> 9, of which waited for: 5 -> 4; matrix products, arithmetic and copies ran while one was open for 5% -> 3% of each run, Pallas kernels for 0% -> 1%
where the time goes in v3:
time: 67.7 us; the launch traced here: 67.2 us
  starting transfers between devices  48.2 us (71%)
  waiting for transfers between devices  11.7 us (17%)
  Pallas kernels  4.34 us (6%)
  local copies, waits for them, and re-layouts  2.01 us (3%)
  between operations  0.88 us (1%)
    ppermute x4, starting transfers between devices, spread_z(): lax.ppermute(value, 'col', [(i, (i + (2 * hops if i % 2 == 0 else -2 * ho...  21.1 us
    ppermute x3, starting transfers between devices, swap_core(): return lax.ppermute(value, 'col', [(i, i ^ 1) for i in range(COLS)])  15 us
    ppermute x1, starting transfers between devices, scatter(): return lax.ppermute(value, ('row', 'col'), perm)  7.52 us
    ppermute x1, waiting for transfers between devices, scatter(): return lax.ppermute(value, ('row', 'col'), perm)  7.08 us
    all_to_all x1, starting transfers between devices, body(): right = lax.all_to_all(fanned, 'row', 0, 0, tiled=True)  4.61 us
    ppermute x4, waiting for transfers between devices, spread_z(): lax.ppermute(value, 'col', [(i, (i + (2 * hops if i % 2 == 0 else -2 * ho...  4.33 us
    pallas_call x1, Pallas kernels, body(): pl.pallas_call(functools.partial(update_kernel, plan), out_shape=blocks,...  3.54 us
  transfers between devices with their start and end apart: 9, of which 4 were waited for; matrix products, arithmetic and copies ran while one was open for 3% of the time, Pallas kernels for 1%

profile of v3, /device:TPU:1, one launch (start us, length us, event | category | flops | bytes accessed | tf_op | source)
XLA Modules:
  0.0 67.2 jit_solution(16362756784577138419)
XLA Ops:
  0.0 8.8 %collective-permute-start = (bf16[4,16,512]{2,1,0:T(8,128)(2,1)}, bf16[4,16,512]{2,1,0:T(8,128)(2,1)S(1)}, u32[]{:S(2)}, u32[]{:S(2)}) collective-permute-start(bf16[4,16,512]{2,1,0:T(8,128)(2,1)} %bitcast.10), channel_id=1, source_target_pairs={{0,1},{1,0},{2,3},{3,2},{4,5},{5,4},{6,7},{7,6},{8,9},{9,8},{10,11... | collective-permute-start | bytes 196616 | tf_op jit(solution)/shard_map/ppermute | solution.py:17
  8.8 0.0 copy-start.3
  8.8 0.8 %dynamic-slice_bitcast_fusion.1 = bf16[1,2,16,512]{3,2,1,0:T(8,128)(2,1)S(1)} fusion(bf16[2,2,16,512]{3,2,1,0:T(8,128)(2,1)} %bitcast.11, s32[]{:T(128)S(6)} %select_n.13), kind=kLoop, calls=%fused_computation.5 | loop fusion | bytes 65540 | tf_op jit(solution)/shard_map/stack | solution.py:114
  9.6 0.2 collective-permute-done
  9.9 0.0 copy-done.3
  9.9 7.1 %collective-permute-start.2 = (bf16[2,4,16,512]{3,2,1,0:T(8,128)(2,1)S(1)}, bf16[2,4,16,512]{3,2,1,0:T(8,128)(2,1)S(1)}, u32[]{:S(2)}, u32[]{:S(2)}) collective-permute-start(bf16[2,4,16,512]{3,2,1,0:T(8,128)(2,1)S(1)} %pad_maximum_fusion.2.refs_0_), channel_id=1, source_target_pairs={{0,8},{1,25},{2,10},{3,27},{4,12},{5,29},{6,14},{7,31},{8,16},{9,1... | collective-permute-start | bytes 393224 | tf_op jit(solution)/shard_map/ppermute | solution.py:21
  17.0 7.5 %collective-permute-start.1 = (bf16[2,2,16,512]{3,2,1,0:T(8,128)(2,1)S(1)}, bf16[2,2,16,512]{3,2,1,0:T(8,128)(2,1)S(1)}, u32[]{:S(2)}, u32[]{:S(2)}) collective-permute-start(bf16[2,2,16,512]{3,2,1,0:T(8,128)(2,1)S(1)} %pad_maximum_fusion.3), channel_id=1, source_target_pairs={{0,320},{1,16},{2,352},{3,112},{4,192},{5,400},{6,416},{7,176},{8,... | collective-permute-start | bytes 196616 | tf_op jit(solution)/shard_map/ppermute | solution.py:49
  24.5 7.1 %collective-permute-done.1 = bf16[2,2,16,512]{3,2,1,0:T(8,128)(2,1)S(1)} collective-permute-done((bf16[2,2,16,512]{3,2,1,0:T(8,128)(2,1)S(1)}, bf16[2,2,16,512]{3,2,1,0:T(8,128)(2,1)S(1)}, u32[]{:S(2)}, u32[]{:S(2)}) %collective-permute-start.1) | collective-permute-done | bytes 65568 | tf_op jit(solution)/shard_map/ppermute | solution.py:49
  31.6 0.0 collective-permute-done.2
  31.6 7.0 %collective-permute-start.3 = (bf16[4,4,16,512]{3,2,1,0:T(8,128)(2,1)S(1)}, bf16[4,4,16,512]{3,2,1,0:T(8,128)(2,1)S(1)}, u32[]{:S(2)}, u32[]{:S(2)}) collective-permute-start(bf16[4,4,16,512]{3,2,1,0:T(8,128)(2,1)S(1)} %pad_maximum_fusion.1), channel_id=1, source_target_pairs={{0,6},{1,27},{2,8},{3,29},{4,10},{5,31},{6,12},{7,1},{8,14},{9,3},... | collective-permute-start | bytes 786440 | tf_op jit(solution)/shard_map/ppermute | solution.py:21
  38.6 1.9 %collective-permute-start.4 = (bf16[4,4,16,512]{3,2,1,0:T(8,128)(2,1)S(1)}, bf16[4,4,16,512]{3,2,1,0:T(8,128)(2,1)S(1)}, u32[]{:S(2)}, u32[]{:S(2)}) collective-permute-start(bf16[4,4,16,512]{3,2,1,0:T(8,128)(2,1)S(1)} %pad_maximum_fusion.1), channel_id=1, source_target_pairs={{0,2},{1,31},{2,4},{3,1},{4,6},{5,3},{6,8},{7,5},{8,10},{9,7},{10,... | collective-permute-start | bytes 786440 | tf_op jit(solution)/shard_map/ppermute | solution.py:21
  40.6 1.1 %broadcast_in_dim.4 = bf16[16,2,2,16,512]{4,3,2,1,0:T(8,128)(2,1)} broadcast(bf16[2,2,16,512]{3,2,1,0:T(8,128)(2,1)S(1)} %collective-permute-done.1), dimensions={1,2,3,4} | broadcast | bytes 1114112 | tf_op jit(solution)/shard_map/broadcast_in_dim | solution.py:121
  41.7 4.6 %all-to-all-start = ((bf16[16,2,2,16,512]{4,3,2,1,0:T(8,128)(2,1)}), bf16[16,2,2,16,512]{4,3,2,1,0:T(8,128)(2,1)S(1)}, u32[]{:S(2)}, u32[]{:S(2)}) async-start(bf16[16,2,2,16,512]{4,3,2,1,0:T(8,128)(2,1)} %broadcast_in_dim.4), calls=%async_computation | async-start | bytes 2097152 | tf_op jit(solution)/shard_map/all_to_all | solution.py:122
  46.3 0.0 collective-permute-done.3
  46.3 2.3 %collective-permute-done.4 = bf16[4,4,16,512]{3,2,1,0:T(8,128)(2,1)S(1)} collective-permute-done((bf16[4,4,16,512]{3,2,1,0:T(8,128)(2,1)S(1)}, bf16[4,4,16,512]{3,2,1,0:T(8,128)(2,1)S(1)}, u32[]{:S(2)}, u32[]{:S(2)}) %collective-permute-start.4) | collective-permute-done | bytes 262176 | tf_op jit(solution)/shard_map/ppermute | solution.py:21
  48.7 0.0 copy-start
  48.7 5.2 %collective-permute-start.5 = (bf16[5,4,16,512]{3,2,1,0:T(8,128)(2,1)S(1)}, bf16[5,4,16,512]{3,2,1,0:T(8,128)(2,1)S(1)}, u32[]{:S(2)}, u32[]{:S(2)}) collective-permute-start(bf16[5,4,16,512]{3,2,1,0:T(8,128)(2,1)S(1)} %pad_maximum_fusion), channel_id=1, source_target_pairs={{0,2},{1,31},{2,4},{3,1},{4,6},{5,3},{6,8},{7,5},{8,10},{9,7},{10,... | collective-permute-start | bytes 983048 | tf_op jit(solution)/shard_map/ppermute | solution.py:21
  53.9 1.9 %collective-permute-start.6 = (bf16[10,4,16,512]{3,2,1,0:T(8,128)(2,1)S(1)}, bf16[10,4,16,512]{3,2,1,0:T(8,128)(2,1)S(1)}, u32[]{:S(2)}, u32[]{:S(2)}) collective-permute-start(bf16[10,4,16,512]{3,2,1,0:T(8,128)(2,1)S(1)} %constant_dynamic-update-slice_fusion.refs_1_), channel_id=1, source_target_pairs={{0,1},{1,0},{2,3},{3,2},{4,5},{5,4},{6,7},{7,6},{8,9},{9,8},{10,11... | collective-permute-start | bytes 1966088 | tf_op jit(solution)/shard_map/ppermute | solution.py:17
  55.8 2.0 %collective-permute-done.5.refs_2_ = bf16[5,4,16,512]{3,2,1,0:T(8,128)(2,1)S(1)} collective-permute-done((bf16[5,4,16,512]{3,2,1,0:T(8,128)(2,1)S(1)}, bf16[5,4,16,512]{3,2,1,0:T(8,128)(2,1)S(1)}, u32[]{:S(2)}, u32[]{:S(2)}) %collective-permute-start.5) | collective-permute-done | bytes 327712 | tf_op jit(solution)/shard_map/ppermute | solution.py:21
  57.9 4.3 %collective-permute-start.7 = (bf16[5,4,16,512]{3,2,1,0:T(8,128)(2,1)S(1)}, bf16[5,4,16,512]{3,2,1,0:T(8,128)(2,1)}, u32[]{:S(2)}, u32[]{:S(2)}) collective-permute-start(bf16[5,4,16,512]{3,2,1,0:T(8,128)(2,1)S(1)} %collective-permute-done.5.refs_2_), channel_id=1, source_target_pairs={{0,1},{1,0},{2,3},{3,2},{4,5},{5,4},{6,7},{7,6},{8,9},{9,8},{10,11... | collective-permute-start | bytes 983048 | tf_op jit(solution)/shard_map/ppermute | solution.py:17
  62.8 0.0 copy-start.1
  62.8 0.0 copy-start.2
  62.8 0.0 all-to-all-done.right_ref
  62.8 0.0 copy-done
  62.8 0.8 %shard_map.55.f_ref = bf16[2,512,512]{2,1,0:T(8,128)(2,1)S(1)} custom-call(bf16[512,512]{1,0:T(8,128)(2,1)S(1)} %copy-done, bf16[16,2,2,16,512]{4,3,2,1,0:T(8,128)(2,1)S(1)} %all-to-all-done.right_ref), custom_call_target="tpu_custom_call" | custom-call | flops 536870912 | bytes 4194304 | tf_op jit(solution)/shard_map/pallas_call | solution.py:144
  63.6 0.0 collective-permute-done.6.refs_3_
  63.6 0.0 collective-permute-done.7.refs_4_
  63.7 0.0 copy-done.1
  63.7 0.0 copy-done.2
  63.7 3.5 %shard_map.56 = bf16[2,512,512]{2,1,0:T(8,128)(2,1)} custom-call(s32[1,1,2]{2,1,0:T(1,128)S(1)} %copy-done.1, s32[1,1,2]{2,1,0:T(1,128)S(1)} %copy-done.2, s32[1,1]{1,0:T(1,128)S(6)} %copy.8.live_ref, bf16[512,512]{1,0:T(8,128)(2,1)S(1)} %copy-done, bf16[2,512,512]{2,1,0:T(8,128)(2,1)S(1)} %shard_map.55.f_ref, ...), custom_call_target="tpu_custom_call" | custom-call | tf_op jit(solution)/shard_map/pallas_call | solution.py:153
  (9 shorter events, 0.1 us)
Async XLA Ops:
  0.0 9.9 %collective-permute-start = (bf16[4,16,512]{2,1,0:T(8,128)(2,1)}, bf16[4,16,512]{2,1,0:T(8,128)(2,1)S(1)}, u32[]{:S(2)}, u32[]{:S(2)}) collective-permute-start(bf16[4,16,512]{2,1,0:T(8,128)(2,1)} %bitcast.10), channel_id=1, source_target_pairs={{0,1},{1,0},{2,3},{3,2},{4,5},{5,4},{6,7},{7,6},{8,9},{9,8},{10,11... | collective-permute-start | bytes 196616 | tf_op jit(solution)/shard_map/ppermute | solution.py:17
  8.8 1.1 %copy-start.3 = (bf16[4,1,16,512]{3,2,1,0:T(8,128)(2,1)S(1)}, bf16[4,1,16,512]{3,2,1,0:T(8,128)(2,1)}, u32[]{:S(2)}) copy-start(bf16[4,1,16,512]{3,2,1,0:T(8,128)(2,1)} %param.5) | copy-start | bytes 196612
  9.9 21.7 %collective-permute-start.2 = (bf16[2,4,16,512]{3,2,1,0:T(8,128)(2,1)S(1)}, bf16[2,4,16,512]{3,2,1,0:T(8,128)(2,1)S(1)}, u32[]{:S(2)}, u32[]{:S(2)}) collective-permute-start(bf16[2,4,16,512]{3,2,1,0:T(8,128)(2,1)S(1)} %pad_maximum_fusion.2.refs_0_), channel_id=1, source_target_pairs={{0,8},{1,25},{2,10},{3,27},{4,12},{5,29},{6,14},{7,31},{8,16},{9,1... | collective-permute-start | bytes 393224 | tf_op jit(solution)/shard_map/ppermute | solution.py:21
  17.0 14.6 %collective-permute-start.1 = (bf16[2,2,16,512]{3,2,1,0:T(8,128)(2,1)S(1)}, bf16[2,2,16,512]{3,2,1,0:T(8,128)(2,1)S(1)}, u32[]{:S(2)}, u32[]{:S(2)}) collective-permute-start(bf16[2,2,16,512]{3,2,1,0:T(8,128)(2,1)S(1)} %pad_maximum_fusion.3), channel_id=1, source_target_pairs={{0,320},{1,16},{2,352},{3,112},{4,192},{5,400},{6,416},{7,176},{8,... | collective-permute-start | bytes 196616 | tf_op jit(solution)/shard_map/ppermute | solution.py:49
  31.6 14.7 %collective-permute-start.3 = (bf16[4,4,16,512]{3,2,1,0:T(8,128)(2,1)S(1)}, bf16[4,4,16,512]{3,2,1,0:T(8,128)(2,1)S(1)}, u32[]{:S(2)}, u32[]{:S(2)}) collective-permute-start(bf16[4,4,16,512]{3,2,1,0:T(8,128)(2,1)S(1)} %pad_maximum_fusion.1), channel_id=1, source_target_pairs={{0,6},{1,27},{2,8},{3,29},{4,10},{5,31},{6,12},{7,1},{8,14},{9,3},... | collective-permute-start | bytes 786440 | tf_op jit(solution)/shard_map/ppermute | solution.py:21
  38.6 10.0 %collective-permute-start.4 = (bf16[4,4,16,512]{3,2,1,0:T(8,128)(2,1)S(1)}, bf16[4,4,16,512]{3,2,1,0:T(8,128)(2,1)S(1)}, u32[]{:S(2)}, u32[]{:S(2)}) collective-permute-start(bf16[4,4,16,512]{3,2,1,0:T(8,128)(2,1)S(1)} %pad_maximum_fusion.1), channel_id=1, source_target_pairs={{0,2},{1,31},{2,4},{3,1},{4,6},{5,3},{6,8},{7,5},{8,10},{9,7},{10,... | collective-permute-start | bytes 786440 | tf_op jit(solution)/shard_map/ppermute | solution.py:21
  41.7 21.1 %all-to-all-start = ((bf16[16,2,2,16,512]{4,3,2,1,0:T(8,128)(2,1)}), bf16[16,2,2,16,512]{4,3,2,1,0:T(8,128)(2,1)S(1)}, u32[]{:S(2)}, u32[]{:S(2)}) async-start(bf16[16,2,2,16,512]{4,3,2,1,0:T(8,128)(2,1)} %broadcast_in_dim.4), calls=%async_computation | async-start | bytes 2097152 | tf_op jit(solution)/shard_map/all_to_all | solution.py:122
  48.7 14.1 %copy-start = (bf16[512,512]{1,0:T(8,128)(2,1)S(1)}, bf16[512,512]{1,0:T(8,128)(2,1)}, u32[]{:S(2)}) copy-start(bf16[512,512]{1,0:T(8,128)(2,1)} %w_ref.3) | copy-start | bytes 1572868
  48.7 9.2 %collective-permute-start.5 = (bf16[5,4,16,512]{3,2,1,0:T(8,128)(2,1)S(1)}, bf16[5,4,16,512]{3,2,1,0:T(8,128)(2,1)S(1)}, u32[]{:S(2)}, u32[]{:S(2)}) collective-permute-start(bf16[5,4,16,512]{3,2,1,0:T(8,128)(2,1)S(1)} %pad_maximum_fusion), channel_id=1, source_target_pairs={{0,2},{1,31},{2,4},{3,1},{4,6},{5,3},{6,8},{7,5},{8,10},{9,7},{10,... | collective-permute-start | bytes 983048 | tf_op jit(solution)/shard_map/ppermute | solution.py:21
  53.9 9.7 %collective-permute-start.6 = (bf16[10,4,16,512]{3,2,1,0:T(8,128)(2,1)S(1)}, bf16[10,4,16,512]{3,2,1,0:T(8,128)(2,1)S(1)}, u32[]{:S(2)}, u32[]{:S(2)}) collective-permute-start(bf16[10,4,16,512]{3,2,1,0:T(8,128)(2,1)S(1)} %constant_dynamic-update-slice_fusion.refs_1_), channel_id=1, source_target_pairs={{0,1},{1,0},{2,3},{3,2},{4,5},{5,4},{6,7},{7,6},{8,9},{9,8},{10,11... | collective-permute-start | bytes 1966088 | tf_op jit(solution)/shard_map/ppermute | solution.py:17
  57.9 5.8 %collective-permute-start.7 = (bf16[5,4,16,512]{3,2,1,0:T(8,128)(2,1)S(1)}, bf16[5,4,16,512]{3,2,1,0:T(8,128)(2,1)}, u32[]{:S(2)}, u32[]{:S(2)}) collective-permute-start(bf16[5,4,16,512]{3,2,1,0:T(8,128)(2,1)S(1)} %collective-permute-done.5.refs_2_), channel_id=1, source_target_pairs={{0,1},{1,0},{2,3},{3,2},{4,5},{5,4},{6,7},{7,6},{8,9},{9,8},{10,11... | collective-permute-start | bytes 983048 | tf_op jit(solution)/shard_map/ppermute | solution.py:17
  62.8 0.9 %copy-start.1 = (s32[1,1,2]{2,1,0:T(1,128)S(1)}, s32[1,1,2]{2,1,0:T(1,128)}, u32[]{:S(2)}) copy-start(s32[1,1,2]{2,1,0:T(1,128)} %rows_ref.1) | copy-start | bytes 28
  62.8 0.9 %copy-start.2 = (s32[1,1,2]{2,1,0:T(1,128)S(1)}, s32[1,1,2]{2,1,0:T(1,128)}, u32[]{:S(2)}) copy-start(s32[1,1,2]{2,1,0:T(1,128)} %cols_ref.1) | copy-start | bytes 28
